TPU v7x, 32 devices: a whole 2x2x4 slice. The times are simulated.
32 devices in a mesh: rows: 16 (over z, y, x), cols: 2 (over core).
Axes of the slice: x: 2, y: 2, z: 4, core: 2. Of those that a mesh axis runs over, the one named last changes fastest.
Arguments:
- quantized: bfloat16 [3072, 384, 128], P('rows', 'cols'), may hold values from 0 to 127, as said below
- scales: bfloat16 [3072, 384], P('rows', 'cols'), may hold values from 0 to 1, as said below
- mode_one: float32 [3072, 32], P('rows'), may hold values from 0 to 40
- mode_two: bfloat16 [384, 32], P('cols'), may hold values from 0 to 1, as said below
- mode_three: bfloat16 [4096, 32], replicated, may hold values from 0 to 0.29882812
- core_tensor: float32 [32, 32, 32], P('rows'), may hold values from 0.0002 to 0.004
- slab_index: int32 [1], replicated, may hold values from 0 to 31
Outputs:
- new_one: float32 [3072, 32], P('rows')
- new_core: float32 [32, 32, 32], P('rows')
Inputs may be any that keep to these rules, and one draw needn't show every extreme that they name: `quantized`: nonnegative integer values of an int8 quantization. `scales`: positive. `mode_two`: nonnegative.
All inputs are finite; a program needn't handle non-finite values.
Results may differ from a plain program's by a relative error of at most 0.0017.
Values sent between devices are 32-bit elements; how exact they have to be, the bound alone decides.
A program may use at most 64 MiB of HBM per device.

v0:
```python
import jax
import jax.numpy as jnp
from jax import lax
from jax.sharding import PartitionSpec as P

SLAB = 128


def weight_gram(core_whole, gram_two, gram_three):
    highest = lax.Precision.HIGHEST
    left = jnp.einsum("rab,ac->rcb", core_whole, gram_two, precision=highest)
    left = jnp.einsum("rcb,bd->rcd", left, gram_three, precision=highest)
    flat = core_whole.reshape(core_whole.shape[0], -1)
    return jnp.dot(left.reshape(flat.shape), flat.T, precision=highest)


def hals_sweep(current, target, coupling):
    highest = lax.Precision.HIGHEST

    def column(position, values):
        where = jnp.asarray(position).astype(jnp.int32)
        weights = lax.dynamic_slice_in_dim(coupling, where, 1, 1)[:, 0]
        diagonal = lax.dynamic_index_in_dim(weights, where, 0, keepdims=False)
        wanted = lax.dynamic_slice_in_dim(target, where, 1, 1)[:, 0]
        before = lax.dynamic_slice_in_dim(values, where, 1, 1)[:, 0]
        fitted = jnp.dot(values, weights, precision=highest)
        after = jnp.maximum(before + (wanted - fitted) / diagonal, 0.0)
        return lax.dynamic_update_slice_in_dim(values, after[:, None], where, 1)

    return lax.fori_loop(0, coupling.shape[0], column, current)


def local(quantized, scales, mode_one, mode_two, mode_three, core_tensor, slab_index):
    highest = lax.Precision.HIGHEST
    whole_core = lax.all_gather(core_tensor, "rows", axis=0, tiled=True)
    flat_core = whole_core.reshape(whole_core.shape[0], -1)
    offset = slab_index[0] * SLAB
    chosen = lax.dynamic_slice_in_dim(mode_three, offset, SLAB, 0)
    tensor = quantized * scales[:, :, None]
    folded = jnp.einsum("jr,ijk->irk", mode_two, tensor, preferred_element_type=jnp.float32).astype(
        jnp.bfloat16
    )
    partial_value = jnp.einsum("irk,ks->irs", folded, chosen, preferred_element_type=jnp.float32)
    partial_value = partial_value.reshape(partial_value.shape[0], -1)
    gram_local = jnp.dot(mode_two.T, mode_two, preferred_element_type=jnp.float32)
    gram_three = jnp.dot(chosen.T, chosen, preferred_element_type=jnp.float32)
    local_target = jnp.dot(partial_value, flat_core.T, precision=highest)
    target, gram_two = lax.psum((local_target, gram_local), "cols")
    coupling = weight_gram(whole_core, gram_two, gram_three)
    updated = hals_sweep(mode_one, target, coupling)
    squares = jnp.sum(updated * updated, axis=0)
    counted = mode_one.shape[0] * lax.axis_size("rows")
    totals = lax.psum(squares, "rows")
    spread = jnp.sqrt(totals / counted + 1e-06)
    normed = updated / spread
    local_rank = core_tensor.shape[0]
    owned = lax.dynamic_slice_in_dim(spread, lax.axis_index("rows") * local_rank, local_rank, 0)
    return (normed, core_tensor * owned[:, None, None])


def solution(mesh):
    in_specs = (
        P("rows", "cols", None),
        P("rows", "cols"),
        P("rows", None),
        P("cols", None),
        P(),
        P("rows", None, None),
        P(),
    )
    out_specs = (P("rows", None), P("rows", None, None))
    return jax.shard_map(local, mesh=mesh, in_specs=in_specs, out_specs=out_specs, check_vma=False)
```

profile of v0, /device:TPU:0, one launch (start us, length us, event | category | flops | bytes accessed | tf_op | source)
XLA Modules:
  0.0 148.8 jit_solution(15536030878287488232)
XLA Ops:
  1.4 8.6 %fusion.10 = bf16[192,32,128]{2,1,0:T(8,128)(2,1)S(1)} fusion(bf16[192,192,128]{2,1,0:T(8,128)(2,1)} %param.9, bf16[192,192]{1,0:T(8,128)(2,1)} %param.10, bf16[192,32]{0,1:T(8,128)(2,1)} %param.12), kind=kOutput, calls=%fused_computation.12 | convolution fusion | flops 321650688 | bytes 11096064 | tf_op jit(solution)/shard_map/jr,ijk->irk/dot_general | solution.py:40
  10.0 1.1 fusion.8
  11.1 45.3 %all_gather.3 = f32[32,32,32]{2,1,0:T(8,128)S(1)} all-gather(f32[2,32,32]{2,1,0:T(8,128)S(1)} %copy-done.2), channel_id=1, replica_groups=mesh['rows'=16,'cols'=2] {'rows'}, dimensions={0}, use_global_device_ids=true | all-gather | bytes 139264 | tf_op jit(solution)/shard_map/all_gather | solution.py:35
  56.5 1.1 convolution_bitcast_fusion.1
  57.7 3.5 %all-reduce = (f32[192,32]{0,1:T(8,128)S(1)}, f32[32,32]{1,0:T(8,128)S(1)}) all-reduce(f32[192,32]{0,1:T(8,128)S(1)} %convolution_bitcast_fusion.1, f32[32,32]{1,0:T(8,128)S(1)} %fusion.24), channel_id=1, replica_groups=mesh['rows'=16,'cols'=2] {'cols'}, use_global_device_ids=true, to_apply=%region_1.0 | all-reduce | flops 7168 | bytes 57344 | tf_op jit(solution)/shard_map/psum | solution.py:48
  62.0 0.9 fusion.13
  62.9 0.8 convolution_bitcast_fusion.2
  63.7 46.9 %while.16 = (s32[]{:T(128)}, f32[192,32]{0,1:T(8,128)S(1)}, f32[192,32]{0,1:T(8,128)S(1)}, f32[32,32]{0,1:T(8,128)S(1)}, s32[]{:T(128)}, /*index=5*/s32[]{:T(128)}, s32[]{:T(128)}) while((s32[]{:T(128)}, f32[192,32]{0,1:T(8,128)S(1)}, f32[192,32]{0,1:T(8,128)S(1)}, f32[32,32]{0,1:T(8,128)S(1)}, s32[]{:T(128)}, /*index=5*/s32[]{:T(128)}, ...), condition=%wide.region_3.4_spmd, body=%wide.region_2.3_spmd.sunk | while | flops 74499 | bytes 41849 | solution.py:30
  64.5 0.7 fusion.37
  65.9 0.7 fusion.37
  67.4 0.7 fusion.37
  68.9 0.7 fusion.37
  76.2 0.7 fusion.37
  77.7 0.7 fusion.37
  79.1 0.7 fusion.37
  89.4 0.7 fusion.37
  90.9 0.7 fusion.37
  92.4 0.7 fusion.37
  104.1 0.7 fusion.37
  105.6 0.7 fusion.37
  107.0 0.7 fusion.37
  110.8 36.6 %psum.23 = f32[32]{0:T(128)S(1)} all-reduce(f32[32]{0:T(128)S(1)} %multiply_reduce_fusion), channel_id=1, replica_groups=mesh['rows'=16,'cols'=2] {'rows'}, use_global_device_ids=true, to_apply=%region_5.6 | all-reduce | flops 32 | bytes 256 | tf_op jit(solution)/shard_map/psum | solution.py:53
  147.4 0.7 broadcast_divide_fusion
  148.1 0.7 broadcast_multiply_fusion
  (161 shorter events, 38.4 us)
Async XLA Ops:
  0.6 9.4 %copy-start = (bf16[4096,32]{0,1:T(8,128)(2,1)S(1)}, bf16[4096,32]{0,1:T(8,128)(2,1)}, u32[]{:S(2)}) copy-start(bf16[4096,32]{0,1:T(8,128)(2,1)} %param.13) | copy-start | bytes 786436
  0.6 56.9 %copy-start.3 = (bf16[192,32]{0,1:T(8,128)(2,1)S(1)}, bf16[192,32]{0,1:T(8,128)(2,1)}, u32[]{:S(2)}) copy-start(bf16[192,32]{0,1:T(8,128)(2,1)} %param.12) | copy-start | bytes 36868
  0.7 10.5 %copy-start.2 = (f32[2,32,32]{2,1,0:T(8,128)S(1)}, f32[2,32,32]{2,1,0:T(8,128)}, u32[]{:S(2)}) copy-start(f32[2,32,32]{2,1,0:T(8,128)} %param.14) | copy-start | bytes 24580
  1.4 62.4 %copy-start.1 = (f32[192,32]{0,1:T(8,128)S(1)}, f32[192,32]{0,1:T(8,128)}, u32[]{:S(2)}) copy-start(f32[192,32]{0,1:T(8,128)} %param.11) | copy-start | bytes 73732
where the time goes:
time: 149 us
  blocking collectives  85.5 us (57%)
  other arithmetic  22.3 us (15%)
  local copies, waits for them, and re-layouts  20.7 us (14%)
  matrix products  17.8 us (12%)
    all_gather x1, blocking collectives, local(): whole_core = lax.all_gather(core_tensor, 'rows', axis=0, tiled=True)  45.3 us
    psum x1, blocking collectives, local(): totals = lax.psum(squares, 'rows')  36.6 us
    max x32, other arithmetic, column(): after = jnp.maximum(before + (wanted - fitted) / diagonal, 0.0)  20.8 us
    dynamic_slice x32, local copies, waits for them, and re-layouts, column(): diagonal = lax.dynamic_index_in_dim(weights, where, 0, keepdims=False)  18.9 us
    dot_general x1, matrix products, local(): jnp.einsum('jr,ijk->irk', mode_two, tensor, preferred_element_type=jnp.fl...  8.62 us
    dot_general x32, matrix products, column(): fitted = jnp.dot(values, weights, precision=highest)  4.4 us
    psum x1, blocking collectives, local(): target, gram_two = lax.psum((local_target, gram_local), 'cols')  3.54 us

commit v1 on v0

--- a/solution.py
+++ b/solution.py
@@ -4,6 +4,27 @@
 from jax.sharding import PartitionSpec as P
 
 SLAB = 128
+
+
+def gather_around(shard, axis, dim):
+    size, index, rows = (lax.axis_size(axis), lax.axis_index(axis), shard.shape[dim])
+    right = [(i, (i + 1) % size) for i in range(size)]
+    left = [(i, (i - 1) % size) for i in range(size)]
+    result = jnp.zeros((*shard.shape[:dim], size * rows, *shard.shape[dim + 1 :]), shard.dtype)
+    result = lax.dynamic_update_slice_in_dim(result, shard, index * rows, axis=dim)
+    from_left = from_right = shard
+    half = size // 2
+    for step in range(1, half + 1):
+        from_left = lax.ppermute(from_left, axis, right)
+        result = lax.dynamic_update_slice_in_dim(
+            result, from_left, (index - step) % size * rows, axis=dim
+        )
+        if step < size - half:
+            from_right = lax.ppermute(from_right, axis, left)
+            result = lax.dynamic_update_slice_in_dim(
+                result, from_right, (index + step) % size * rows, axis=dim
+            )
+    return result
 
 
 def weight_gram(core_whole, gram_two, gram_three):
@@ -32,7 +53,7 @@
 
 def local(quantized, scales, mode_one, mode_two, mode_three, core_tensor, slab_index):
     highest = lax.Precision.HIGHEST
-    whole_core = lax.all_gather(core_tensor, "rows", axis=0, tiled=True)
+    whole_core = gather_around(core_tensor, "rows", 0)
     flat_core = whole_core.reshape(whole_core.shape[0], -1)
     offset = slab_index[0] * SLAB
     chosen = lax.dynamic_slice_in_dim(mode_three, offset, SLAB, 0)

time: 149 us -> 164 us (1.10)
  blocking collectives: 85.5 us -> 40.1 us
  starting transfers between devices: 0 us -> 41 us
  waiting for transfers between devices: 0 us -> 18 us
    all_gather x1 -> x0, blocking collectives: 45.3 us -> none  [local(): whole_core = lax.all_gather(core_tensor, 'rows', axis=0, tiled=True)]
    ppermute x0 -> x15, starting transfers between devices: none -> 41 us  [the longest x7 37.9 us: gather_around(): from_right = lax.ppermute(from_right, axis, left)]
    ppermute x0 -> x15, waiting for transfers between devices: none -> 18 us  [the longest x8 18 us: gather_around(): from_left = lax.ppermute(from_left, axis, right)]
  transfers between devices with their start and end apart: 0 -> 15, of which waited for: 0 -> 7; matrix products, arithmetic and copies ran while one was open for 0% -> 7% of each run, Pallas kernels for 0% -> 0%
where the time goes in v1:
time: 164 us
  starting transfers between devices  41 us (25%)
  blocking collectives  40.1 us (24%)
  other arithmetic  22.3 us (14%)
  local copies, waits for them, and re-layouts  21.4 us (13%)
  matrix products  18.1 us (11%)
  waiting for transfers between devices  18 us (11%)
  between operations  1.67 us (1%)
    ppermute x7, starting transfers between devices, gather_around(): from_right = lax.ppermute(from_right, axis, left)  37.9 us
    psum x1, blocking collectives, local(): totals = lax.psum(squares, 'rows')  36.6 us
    max x32, other arithmetic, column(): after = jnp.maximum(before + (wanted - fitted) / diagonal, 0.0)  20.8 us
    dynamic_slice x32, local copies, waits for them, and re-layouts, column(): diagonal = lax.dynamic_index_in_dim(weights, where, 0, keepdims=False)  18.9 us
    ppermute x8, waiting for transfers between devices, gather_around(): from_left = lax.ppermute(from_left, axis, right)  18 us
    dot_general x1, matrix products, local(): jnp.einsum('jr,ijk->irk', mode_two, tensor, preferred_element_type=jnp.fl...  8.47 us
    dot_general x32, matrix products, column(): fitted = jnp.dot(values, weights, precision=highest)  4.4 us
    psum x1, blocking collectives, local(): target, gram_two = lax.psum((local_target, gram_local), 'cols')  3.54 us
  transfers between devices with their start and end apart: 15, of which 7 were waited for; matrix products, arithmetic and copies ran while one was open for 7% of the time, Pallas kernels for 0%

profile of v1, /device:TPU:0, one launch (start us, length us, event | category | flops | bytes accessed | tf_op | source)
XLA Modules:
  0.0 163.7 jit_solution(6970327757383597851)
XLA Ops:
  0.7 3.0 %collective-permute-start = (f32[2,32,32]{2,1,0:T(8,128)}, f32[2,32,32]{2,1,0:T(8,128)S(1)}, u32[]{:S(2)}, u32[]{:S(2)}) collective-permute-start(f32[2,32,32]{2,1,0:T(8,128)} %param.14), channel_id=1, source_target_pairs={{0,2},{2,4},{4,6},{6,8},{8,10},{10,12},{12,14},{14,16},{16,18},{18... | collective-permute-start | bytes 24584 | tf_op jit(solution)/shard_map/ppermute | solution.py:18
  3.6 4.1 %collective-permute-start.1 = (f32[2,32,32]{2,1,0:T(8,128)}, f32[2,32,32]{2,1,0:T(8,128)S(1)}, u32[]{:S(2)}, u32[]{:S(2)}) collective-permute-start(f32[2,32,32]{2,1,0:T(8,128)} %param.14), channel_id=1, source_target_pairs={{0,30},{2,0},{4,2},{6,4},{8,6},{10,8},{12,10},{14,12},{16,14},{18,... | collective-permute-start | bytes 24584 | tf_op jit(solution)/shard_map/ppermute | solution.py:23
  8.4 0.9 fusion.23
  9.3 8.5 %fusion.10 = bf16[192,32,128]{2,1,0:T(8,128)(2,1)S(1)} fusion(bf16[192,192,128]{2,1,0:T(8,128)(2,1)} %param.9, bf16[192,192]{1,0:T(8,128)(2,1)} %param.10, bf16[192,32]{0,1:T(8,128)(2,1)} %param.12), kind=kOutput, calls=%fused_computation.12 | convolution fusion | flops 321650688 | bytes 11096064 | tf_op jit(solution)/shard_map/jr,ijk->irk/dot_general | solution.py:61
  17.9 1.1 fusion.8
  19.3 5.6 %collective-permute-start.3 = (f32[2,32,32]{2,1,0:T(8,128)S(1)}, f32[2,32,32]{2,1,0:T(8,128)S(1)}, u32[]{:S(2)}, u32[]{:S(2)}) collective-permute-start(f32[2,32,32]{2,1,0:T(8,128)S(1)} %collective-permute-done.1), channel_id=1, source_target_pairs={{0,30},{2,0},{4,2},{6,4},{8,6},{10,8},{12,10},{14,12},{16,14},{18,... | collective-permute-start | bytes 24584 | tf_op jit(solution)/shard_map/ppermute | solution.py:23
  25.0 1.8 %collective-permute-done.2 = f32[2,32,32]{2,1,0:T(8,128)S(1)} collective-permute-done((f32[2,32,32]{2,1,0:T(8,128)S(1)}, f32[2,32,32]{2,1,0:T(8,128)S(1)}, u32[]{:S(2)}, u32[]{:S(2)}) %collective-permute-start.2) | collective-permute-done | bytes 8224 | tf_op jit(solution)/shard_map/ppermute | solution.py:18
  26.8 5.6 %collective-permute-start.5 = (f32[2,32,32]{2,1,0:T(8,128)S(1)}, f32[2,32,32]{2,1,0:T(8,128)S(1)}, u32[]{:S(2)}, u32[]{:S(2)}) collective-permute-start(f32[2,32,32]{2,1,0:T(8,128)S(1)} %collective-permute-done.3), channel_id=1, source_target_pairs={{0,30},{2,0},{4,2},{6,4},{8,6},{10,8},{12,10},{14,12},{16,14},{18,... | collective-permute-start | bytes 24584 | tf_op jit(solution)/shard_map/ppermute | solution.py:23
  32.5 1.8 %collective-permute-done.4 = f32[2,32,32]{2,1,0:T(8,128)S(1)} collective-permute-done((f32[2,32,32]{2,1,0:T(8,128)S(1)}, f32[2,32,32]{2,1,0:T(8,128)S(1)}, u32[]{:S(2)}, u32[]{:S(2)}) %collective-permute-start.4) | collective-permute-done | bytes 8224 | tf_op jit(solution)/shard_map/ppermute | solution.py:18
  34.3 5.6 %collective-permute-start.7 = (f32[2,32,32]{2,1,0:T(8,128)S(1)}, f32[2,32,32]{2,1,0:T(8,128)S(1)}, u32[]{:S(2)}, u32[]{:S(2)}) collective-permute-start(f32[2,32,32]{2,1,0:T(8,128)S(1)} %collective-permute-done.5), channel_id=1, source_target_pairs={{0,30},{2,0},{4,2},{6,4},{8,6},{10,8},{12,10},{14,12},{16,14},{18,... | collective-permute-start | bytes 24584 | tf_op jit(solution)/shard_map/ppermute | solution.py:23
  40.0 1.8 %collective-permute-done.6 = f32[2,32,32]{2,1,0:T(8,128)S(1)} collective-permute-done((f32[2,32,32]{2,1,0:T(8,128)S(1)}, f32[2,32,32]{2,1,0:T(8,128)S(1)}, u32[]{:S(2)}, u32[]{:S(2)}) %collective-permute-start.6) | collective-permute-done | bytes 8224 | tf_op jit(solution)/shard_map/ppermute | solution.py:18
  41.8 5.6 %collective-permute-start.9 = (f32[2,32,32]{2,1,0:T(8,128)S(1)}, f32[2,32,32]{2,1,0:T(8,128)S(1)}, u32[]{:S(2)}, u32[]{:S(2)}) collective-permute-start(f32[2,32,32]{2,1,0:T(8,128)S(1)} %collective-permute-done.7), channel_id=1, source_target_pairs={{0,30},{2,0},{4,2},{6,4},{8,6},{10,8},{12,10},{14,12},{16,14},{18,... | collective-permute-start | bytes 24584 | tf_op jit(solution)/shard_map/ppermute | solution.py:23
  47.5 1.8 %collective-permute-done.8 = f32[2,32,32]{2,1,0:T(8,128)S(1)} collective-permute-done((f32[2,32,32]{2,1,0:T(8,128)S(1)}, f32[2,32,32]{2,1,0:T(8,128)S(1)}, u32[]{:S(2)}, u32[]{:S(2)}) %collective-permute-start.8) | collective-permute-done | bytes 8224 | tf_op jit(solution)/shard_map/ppermute | solution.py:18
  49.3 5.6 %collective-permute-start.11 = (f32[2,32,32]{2,1,0:T(8,128)S(1)}, f32[2,32,32]{2,1,0:T(8,128)S(1)}, u32[]{:S(2)}, u32[]{:S(2)}) collective-permute-start(f32[2,32,32]{2,1,0:T(8,128)S(1)} %collective-permute-done.9), channel_id=1, source_target_pairs={{0,30},{2,0},{4,2},{6,4},{8,6},{10,8},{12,10},{14,12},{16,14},{18,... | collective-permute-start | bytes 24584 | tf_op jit(solution)/shard_map/ppermute | solution.py:23
  55.1 1.8 %collective-permute-done.10 = f32[2,32,32]{2,1,0:T(8,128)S(1)} collective-permute-done((f32[2,32,32]{2,1,0:T(8,128)S(1)}, f32[2,32,32]{2,1,0:T(8,128)S(1)}, u32[]{:S(2)}, u32[]{:S(2)}) %collective-permute-start.10) | collective-permute-done | bytes 8224 | tf_op jit(solution)/shard_map/ppermute | solution.py:18
  56.9 5.8 %collective-permute-start.13 = (f32[2,32,32]{2,1,0:T(8,128)S(1)}, f32[2,32,32]{2,1,0:T(8,128)S(1)}, u32[]{:S(2)}, u32[]{:S(2)}) collective-permute-start(f32[2,32,32]{2,1,0:T(8,128)S(1)} %collective-permute-done.11), channel_id=1, source_target_pairs={{0,30},{2,0},{4,2},{6,4},{8,6},{10,8},{12,10},{14,12},{16,14},{18,... | collective-permute-start | bytes 24584 | tf_op jit(solution)/shard_map/ppermute | solution.py:23
  62.7 1.6 collective-permute-done.12
  64.5 7.4 %collective-permute-done.14 = f32[2,32,32]{2,1,0:T(8,128)S(1)} collective-permute-done((f32[2,32,32]{2,1,0:T(8,128)S(1)}, f32[2,32,32]{2,1,0:T(8,128)S(1)}, u32[]{:S(2)}, u32[]{:S(2)}) %collective-permute-start.14) | collective-permute-done | bytes 8224 | tf_op jit(solution)/shard_map/ppermute | solution.py:18
  71.9 0.8 convolution_bitcast_fusion.1
  72.8 3.5 %all-reduce = (f32[192,32]{0,1:T(8,128)S(1)}, f32[32,32]{1,0:T(8,128)S(1)}) all-reduce(f32[192,32]{0,1:T(8,128)S(1)} %convolution_bitcast_fusion.1, f32[32,32]{1,0:T(8,128)S(1)} %fusion.23), channel_id=1, replica_groups=mesh['rows'=16,'cols'=2] {'cols'}, use_global_device_ids=true, to_apply=%region_1.2 | all-reduce | flops 7168 | bytes 57344 | tf_op jit(solution)/shard_map/psum | solution.py:69
  76.3 0.9 convolution_bitcast_fusion
  77.2 0.9 fusion.13
  78.6 46.9 %while.16 = (s32[]{:T(128)}, f32[192,32]{0,1:T(8,128)S(1)}, f32[192,32]{0,1:T(8,128)S(1)}, f32[32,32]{0,1:T(8,128)S(1)}, s32[]{:T(128)}, /*index=5*/s32[]{:T(128)}, s32[]{:T(128)}) while((s32[]{:T(128)}, f32[192,32]{0,1:T(8,128)S(1)}, f32[192,32]{0,1:T(8,128)S(1)}, f32[32,32]{0,1:T(8,128)S(1)}, s32[]{:T(128)}, /*index=5*/s32[]{:T(128)}, ...), condition=%wide.region_3.4_spmd, body=%wide.region_2.3_spmd.sunk | while | flops 74499 | bytes 41857 | solution.py:51
  125.7 36.6 %psum.23 = f32[32]{0:T(128)S(1)} all-reduce(f32[32]{0:T(128)S(1)} %multiply_reduce_fusion), channel_id=1, replica_groups=mesh['rows'=16,'cols'=2] {'rows'}, use_global_device_ids=true, to_apply=%region_5.6 | all-reduce | flops 32 | bytes 256 | tf_op jit(solution)/shard_map/psum | solution.py:74
  (205 shorter events, 48.9 us)
Async XLA Ops:
  0.6 17.3 %copy-start = (bf16[4096,32]{0,1:T(8,128)(2,1)S(1)}, bf16[4096,32]{0,1:T(8,128)(2,1)}, u32[]{:S(2)}) copy-start(bf16[4096,32]{0,1:T(8,128)(2,1)} %param.13) | copy-start | bytes 786436
  0.6 17.2 %copy-start.2 = (f32[2,32,32]{2,1,0:T(8,128)S(1)}, f32[2,32,32]{2,1,0:T(8,128)}, u32[]{:S(2)}) copy-start(f32[2,32,32]{2,1,0:T(8,128)} %param.14) | copy-start | bytes 24580
  0.7 18.6 %collective-permute-start = (f32[2,32,32]{2,1,0:T(8,128)}, f32[2,32,32]{2,1,0:T(8,128)S(1)}, u32[]{:S(2)}, u32[]{:S(2)}) collective-permute-start(f32[2,32,32]{2,1,0:T(8,128)} %param.14), channel_id=1, source_target_pairs={{0,2},{2,4},{4,6},{6,8},{8,10},{10,12},{12,14},{14,16},{16,18},{18... | collective-permute-start | bytes 24584 | tf_op jit(solution)/shard_map/ppermute | solution.py:18
  3.6 15.6 %collective-permute-start.1 = (f32[2,32,32]{2,1,0:T(8,128)}, f32[2,32,32]{2,1,0:T(8,128)S(1)}, u32[]{:S(2)}, u32[]{:S(2)}) collective-permute-start(f32[2,32,32]{2,1,0:T(8,128)} %param.14), channel_id=1, source_target_pairs={{0,30},{2,0},{4,2},{6,4},{8,6},{10,8},{12,10},{14,12},{16,14},{18,... | collective-permute-start | bytes 24584 | tf_op jit(solution)/shard_map/ppermute | solution.py:23
  9.3 69.4 %copy-start.1 = (f32[192,32]{0,1:T(8,128)S(1)}, f32[192,32]{0,1:T(8,128)}, u32[]{:S(2)}) copy-start(f32[192,32]{0,1:T(8,128)} %param.11) | copy-start | bytes 73732
  19.3 7.5 %collective-permute-start.2 = (f32[2,32,32]{2,1,0:T(8,128)S(1)}, f32[2,32,32]{2,1,0:T(8,128)S(1)}, u32[]{:S(2)}, u32[]{:S(2)}) collective-permute-start(f32[2,32,32]{2,1,0:T(8,128)S(1)} %collective-permute-done), channel_id=1, source_target_pairs={{0,2},{2,4},{4,6},{6,8},{8,10},{10,12},{12,14},{14,16},{16,18},{18... | collective-permute-start | bytes 24584 | tf_op jit(solution)/shard_map/ppermute | solution.py:18
  19.3 7.5 %collective-permute-start.3 = (f32[2,32,32]{2,1,0:T(8,128)S(1)}, f32[2,32,32]{2,1,0:T(8,128)S(1)}, u32[]{:S(2)}, u32[]{:S(2)}) collective-permute-start(f32[2,32,32]{2,1,0:T(8,128)S(1)} %collective-permute-done.1), channel_id=1, source_target_pairs={{0,30},{2,0},{4,2},{6,4},{8,6},{10,8},{12,10},{14,12},{16,14},{18,... | collective-permute-start | bytes 24584 | tf_op jit(solution)/shard_map/ppermute | solution.py:23
  26.8 7.5 %collective-permute-start.4 = (f32[2,32,32]{2,1,0:T(8,128)S(1)}, f32[2,32,32]{2,1,0:T(8,128)S(1)}, u32[]{:S(2)}, u32[]{:S(2)}) collective-permute-start(f32[2,32,32]{2,1,0:T(8,128)S(1)} %collective-permute-done.2), channel_id=1, source_target_pairs={{0,2},{2,4},{4,6},{6,8},{8,10},{10,12},{12,14},{14,16},{16,18},{18... | collective-permute-start | bytes 24584 | tf_op jit(solution)/shard_map/ppermute | solution.py:18
  26.8 7.5 %collective-permute-start.5 = (f32[2,32,32]{2,1,0:T(8,128)S(1)}, f32[2,32,32]{2,1,0:T(8,128)S(1)}, u32[]{:S(2)}, u32[]{:S(2)}) collective-permute-start(f32[2,32,32]{2,1,0:T(8,128)S(1)} %collective-permute-done.3), channel_id=1, source_target_pairs={{0,30},{2,0},{4,2},{6,4},{8,6},{10,8},{12,10},{14,12},{16,14},{18,... | collective-permute-start | bytes 24584 | tf_op jit(solution)/shard_map/ppermute | solution.py:23
  34.3 7.5 %collective-permute-start.6 = (f32[2,32,32]{2,1,0:T(8,128)S(1)}, f32[2,32,32]{2,1,0:T(8,128)S(1)}, u32[]{:S(2)}, u32[]{:S(2)}) collective-permute-start(f32[2,32,32]{2,1,0:T(8,128)S(1)} %collective-permute-done.4), channel_id=1, source_target_pairs={{0,2},{2,4},{4,6},{6,8},{8,10},{10,12},{12,14},{14,16},{16,18},{18... | collective-permute-start | bytes 24584 | tf_op jit(solution)/shard_map/ppermute | solution.py:18
  34.3 7.5 %collective-permute-start.7 = (f32[2,32,32]{2,1,0:T(8,128)S(1)}, f32[2,32,32]{2,1,0:T(8,128)S(1)}, u32[]{:S(2)}, u32[]{:S(2)}) collective-permute-start(f32[2,32,32]{2,1,0:T(8,128)S(1)} %collective-permute-done.5), channel_id=1, source_target_pairs={{0,30},{2,0},{4,2},{6,4},{8,6},{10,8},{12,10},{14,12},{16,14},{18,... | collective-permute-start | bytes 24584 | tf_op jit(solution)/shard_map/ppermute | solution.py:23
  41.8 7.5 %collective-permute-start.8 = (f32[2,32,32]{2,1,0:T(8,128)S(1)}, f32[2,32,32]{2,1,0:T(8,128)S(1)}, u32[]{:S(2)}, u32[]{:S(2)}) collective-permute-start(f32[2,32,32]{2,1,0:T(8,128)S(1)} %collective-permute-done.6), channel_id=1, source_target_pairs={{0,2},{2,4},{4,6},{6,8},{8,10},{10,12},{12,14},{14,16},{16,18},{18... | collective-permute-start | bytes 24584 | tf_op jit(solution)/shard_map/ppermute | solution.py:18
  41.8 7.5 %collective-permute-start.9 = (f32[2,32,32]{2,1,0:T(8,128)S(1)}, f32[2,32,32]{2,1,0:T(8,128)S(1)}, u32[]{:S(2)}, u32[]{:S(2)}) collective-permute-start(f32[2,32,32]{2,1,0:T(8,128)S(1)} %collective-permute-done.7), channel_id=1, source_target_pairs={{0,30},{2,0},{4,2},{6,4},{8,6},{10,8},{12,10},{14,12},{16,14},{18,... | collective-permute-start | bytes 24584 | tf_op jit(solution)/shard_map/ppermute | solution.py:23
  49.3 7.5 %collective-permute-start.10 = (f32[2,32,32]{2,1,0:T(8,128)S(1)}, f32[2,32,32]{2,1,0:T(8,128)S(1)}, u32[]{:S(2)}, u32[]{:S(2)}) collective-permute-start(f32[2,32,32]{2,1,0:T(8,128)S(1)} %collective-permute-done.8), channel_id=1, source_target_pairs={{0,2},{2,4},{4,6},{6,8},{8,10},{10,12},{12,14},{14,16},{16,18},{18... | collective-permute-start | bytes 24584 | tf_op jit(solution)/shard_map/ppermute | solution.py:18
  49.3 7.5 %collective-permute-start.11 = (f32[2,32,32]{2,1,0:T(8,128)S(1)}, f32[2,32,32]{2,1,0:T(8,128)S(1)}, u32[]{:S(2)}, u32[]{:S(2)}) collective-permute-start(f32[2,32,32]{2,1,0:T(8,128)S(1)} %collective-permute-done.9), channel_id=1, source_target_pairs={{0,30},{2,0},{4,2},{6,4},{8,6},{10,8},{12,10},{14,12},{16,14},{18,... | collective-permute-start | bytes 24584 | tf_op jit(solution)/shard_map/ppermute | solution.py:23
  56.8 7.5 %collective-permute-start.12 = (f32[2,32,32]{2,1,0:T(8,128)S(1)}, f32[2,32,32]{2,1,0:T(8,128)S(1)}, u32[]{:S(2)}, u32[]{:S(2)}) collective-permute-start(f32[2,32,32]{2,1,0:T(8,128)S(1)} %collective-permute-done.10), channel_id=1, source_target_pairs={{0,2},{2,4},{4,6},{6,8},{8,10},{10,12},{12,14},{14,16},{16,18},{18... | collective-permute-start | bytes 24584 | tf_op jit(solution)/shard_map/ppermute | solution.py:18
  56.9 7.6 %collective-permute-start.13 = (f32[2,32,32]{2,1,0:T(8,128)S(1)}, f32[2,32,32]{2,1,0:T(8,128)S(1)}, u32[]{:S(2)}, u32[]{:S(2)}) collective-permute-start(f32[2,32,32]{2,1,0:T(8,128)S(1)} %collective-permute-done.11), channel_id=1, source_target_pairs={{0,30},{2,0},{4,2},{6,4},{8,6},{10,8},{12,10},{14,12},{16,14},{18,... | collective-permute-start | bytes 24584 | tf_op jit(solution)/shard_map/ppermute | solution.py:23
  64.4 7.5 %collective-permute-start.14 = (f32[2,32,32]{2,1,0:T(8,128)S(1)}, f32[2,32,32]{2,1,0:T(8,128)S(1)}, u32[]{:S(2)}, u32[]{:S(2)}) collective-permute-start(f32[2,32,32]{2,1,0:T(8,128)S(1)} %collective-permute-done.12), channel_id=1, source_target_pairs={{0,2},{2,4},{4,6},{6,8},{8,10},{10,12},{12,14},{14,16},{16,18},{18... | collective-permute-start | bytes 24584 | tf_op jit(solution)/shard_map/ppermute | solution.py:18
